TPU v7x, 128 devices: a whole 4x4x4 slice. The times are simulated.
128 devices in a mesh: pr: 16 (over z, x), pc: 8 (over y, core).
Axes of the slice: x: 4, y: 4, z: 4, core: 2. Of those that a mesh axis runs over, the one named last changes fastest.
Arguments:
- trailing: float32 [20480, 20480], P('pr', 'pc'), may hold values from -25 to 25, as said below
- v_panels: float32 [6, 32, 20480], P(None, None, ('pr', 'pc')), may hold values from -0.078125 to 0.078125
- t_panels: float32 [6, 32, 32], replicated, may hold values from -0.2 to 0.5, as said below
Outputs:
- updated: float32 [20480, 20480], P('pr', 'pc')
- w_panels: float32 [6, 32, 20480], P(None, None, ('pr', 'pc'))
Inputs may be any that keep to these rules, and one draw needn't show every extreme that they name: trailing is exactly symmetric. `t_panels`: each panel's factor is upper triangular with diagonal entries of 0.25 to 0.5.
All inputs are finite; a program needn't handle non-finite values.
Results may differ from a plain program's by a relative error of at most 0.00013.
Values sent between devices are 32-bit elements; how exact they have to be, the bound alone decides.
A program may use at most 128 MiB of HBM per device.

v0:
```python
import jax
import jax.numpy as jnp
from jax import lax
from jax.sharding import PartitionSpec as P


def broadcast(value, axis, source):
    kept = jnp.where(lax.axis_index(axis) == source, value, 0).astype(value.dtype)
    return lax.psum(kept, axis)


def contract(left_side, right_side, left_dim, right_dim):
    return lax.dot_general(
        left_side,
        right_side,
        (((left_dim,), (right_dim,)), ((), ())),
        precision=lax.Precision.HIGHEST,
        preferred_element_type=jnp.float32,
    )


def fetch_v_columns(v_row, col_rank, ratio):
    pieces = []
    for offset in range(ratio):
        pieces.append(broadcast(v_row, "pr", col_rank * ratio + offset))
    return jnp.concatenate(pieces, axis=1)


def fetch_w_columns(w_row, col_rank, ratio):
    pieces = []
    for offset in range(ratio):
        pieces.append(broadcast(w_row, "pr", col_rank * ratio + offset))
    return jnp.concatenate(pieces, axis=1)


def per_device(trailing, v_panels, t_panels):
    matrix = trailing
    rows_here = matrix.shape[0]
    col_rank = lax.axis_index("pc")
    ratio = lax.axis_size("pr") // lax.axis_size("pc")
    share = rows_here // lax.axis_size("pc")
    w_blocks = []
    for panel in range(v_panels.shape[0]):
        v_row = lax.all_gather(v_panels[panel], "pc", axis=1, tiled=True)
        v_col = fetch_v_columns(v_row, col_rank, ratio)
        factor = t_panels[panel]
        partial_value = contract(v_col, matrix, 1, 1)
        x_row = lax.psum(partial_value, "pc")
        gram_block = lax.psum(contract(v_row, x_row, 1, 1), "pr")
        middle = contract(contract(factor, gram_block, 0, 0), factor, 1, 0)
        w_row = contract(factor, x_row, 0, 0) - 0.5 * contract(middle, v_row, 0, 0)
        w_col = fetch_w_columns(w_row, col_rank, ratio)
        left_side = jnp.concatenate([v_row, w_row], axis=0)
        right_side = jnp.concatenate([w_col, v_col], axis=0)
        matrix = matrix - contract(left_side, right_side, 0, 0)
        w_blocks.append(lax.dynamic_slice_in_dim(w_row, col_rank * share, share, 1))
    return (matrix, jnp.stack(w_blocks))


def solution(mesh):
    return jax.shard_map(
        per_device,
        mesh=mesh,
        in_specs=(P("pr", "pc"), P(None, None, ("pr", "pc")), P()),
        out_specs=(P("pr", "pc"), P(None, None, ("pr", "pc"))),
        check_vma=False,
    )
```

profile of v0, /device:TPU:0, one launch (start us, length us, event | category | flops | bytes accessed | tf_op | source)
XLA Modules:
  0.0 1610.5 jit_solution(2257900202977496059)
XLA Ops:
  36.9 71.9 %all-reduce.45.cloned.1.call-done = (f32[32,1280]{1,0:T(8,128)}, f32[32,1280]{1,0:T(8,128)}) async-done(((f32[32,1280]{1,0:T(8,128)}, f32[32,1280]{1,0:T(8,128)}), (f32[32,1280]{1,0:T(8,128)}, f32[32,1280]{1,0:T(8,128)})) %all-reduce.45.cloned.1.call-update) | async-done | bytes 327696 | tf_op jit(solution)/shard_map/psum | solution.py:9
  110.6 15.3 fusion.109
  126.8 56.5 %all-reduce.21.cloned.1.call-done = f32[32,1280]{1,0:T(8,128)} async-done(((f32[32,1280]{1,0:T(8,128)}), f32[32,1280]{1,0:T(8,128)}) %all-reduce.21.cloned.1.call-update) | async-done | bytes 163856 | tf_op jit(solution)/shard_map/psum | solution.py:48
  184.6 74.6 %psum.255 = f32[32,32]{0,1:T(8,128)S(1)} all-reduce(f32[32,32]{0,1:T(8,128)S(1)} %convolution_bitcast_fusion.11), channel_id=1, replica_groups=mesh['pr'=16,'pc'=8] {'pr'}, use_global_device_ids=true, to_apply=%region_3.4 | all-reduce | flops 1024 | bytes 8192 | tf_op jit(solution)/shard_map/psum | solution.py:49
  276.3 65.5 %all-reduce.43.cloned.1.call-done = (f32[32,1280]{1,0:T(8,128)}, f32[32,1280]{1,0:T(8,128)}, f32[32,1280]{1,0:T(8,128)}, f32[32,1280]{1,0:T(8,128)}) async-done(((f32[32,1280]{1,0:T(8,128)}, f32[32,1280]{1,0:T(8,128)}, f32[32,1280]{1,0:T(8,128)}, f32[32,1280]{1,0:T(8,128)}), (f32[32,1280]{1,0:T(8,128)}, f32[32,1280]{1,0:T(8,128)}, f32[32,1280]{1,0:T(8,128)}, ...) | async-done | bytes 655376 | tf_op jit(solution)/shard_map/psum | solution.py:9
  343.7 14.6 convolution_subtract_fusion.5
  376.5 56.5 %all-reduce.23.cloned.1.call-done = f32[32,1280]{1,0:T(8,128)} async-done(((f32[32,1280]{1,0:T(8,128)}), f32[32,1280]{1,0:T(8,128)}) %all-reduce.23.cloned.1.call-update) | async-done | bytes 163856 | tf_op jit(solution)/shard_map/psum | solution.py:48
  434.4 74.6 %psum.261 = f32[32,32]{0,1:T(8,128)S(1)} all-reduce(f32[32,32]{0,1:T(8,128)S(1)} %convolution_bitcast_fusion.10), channel_id=1, replica_groups=mesh['pr'=16,'pc'=8] {'pr'}, use_global_device_ids=true, to_apply=%region_9.10 | all-reduce | flops 1024 | bytes 8192 | tf_op jit(solution)/shard_map/psum | solution.py:49
  537.6 54.1 %all-reduce.41.cloned.1.call-done = (f32[32,1280]{1,0:T(8,128)}, f32[32,1280]{1,0:T(8,128)}, f32[32,1280]{1,0:T(8,128)}, f32[32,1280]{1,0:T(8,128)}) async-done(((f32[32,1280]{1,0:T(8,128)}, f32[32,1280]{1,0:T(8,128)}, f32[32,1280]{1,0:T(8,128)}, f32[32,1280]{1,0:T(8,128)}), (f32[32,1280]{1,0:T(8,128)}, f32[32,1280]{1,0:T(8,128)}, f32[32,1280]{1,0:T(8,128)}, ...) | async-done | bytes 655376 | tf_op jit(solution)/shard_map/psum | solution.py:9
  626.0 56.5 %all-reduce.25.cloned.1.call-done = f32[32,1280]{1,0:T(8,128)} async-done(((f32[32,1280]{1,0:T(8,128)}), f32[32,1280]{1,0:T(8,128)}) %all-reduce.25.cloned.1.call-update) | async-done | bytes 163856 | tf_op jit(solution)/shard_map/psum | solution.py:48
  683.9 74.6 %psum.267 = f32[32,32]{0,1:T(8,128)S(1)} all-reduce(f32[32,32]{0,1:T(8,128)S(1)} %convolution_bitcast_fusion.9), channel_id=1, replica_groups=mesh['pr'=16,'pc'=8] {'pr'}, use_global_device_ids=true, to_apply=%region_15.16 | all-reduce | flops 1024 | bytes 8192 | tf_op jit(solution)/shard_map/psum | solution.py:49
  775.7 65.4 %all-reduce.39.cloned.1.call-done = (f32[32,1280]{1,0:T(8,128)}, f32[32,1280]{1,0:T(8,128)}, f32[32,1280]{1,0:T(8,128)}, f32[32,1280]{1,0:T(8,128)}) async-done(((f32[32,1280]{1,0:T(8,128)}, f32[32,1280]{1,0:T(8,128)}, f32[32,1280]{1,0:T(8,128)}, f32[32,1280]{1,0:T(8,128)}), (f32[32,1280]{1,0:T(8,128)}, f32[32,1280]{1,0:T(8,128)}, f32[32,1280]{1,0:T(8,128)}, ...) | async-done | bytes 655376 | tf_op jit(solution)/shard_map/psum | solution.py:9
  843.0 14.2 convolution_subtract_fusion.3
  875.5 56.5 %all-reduce.27.cloned.1.call-done = f32[32,1280]{1,0:T(8,128)} async-done(((f32[32,1280]{1,0:T(8,128)}), f32[32,1280]{1,0:T(8,128)}) %all-reduce.27.cloned.1.call-update) | async-done | bytes 163856 | tf_op jit(solution)/shard_map/psum | solution.py:48
  933.4 74.6 %psum.273 = f32[32,32]{0,1:T(8,128)S(1)} all-reduce(f32[32,32]{0,1:T(8,128)S(1)} %convolution_bitcast_fusion.8), channel_id=1, replica_groups=mesh['pr'=16,'pc'=8] {'pr'}, use_global_device_ids=true, to_apply=%region_21.22 | all-reduce | flops 1024 | bytes 8192 | tf_op jit(solution)/shard_map/psum | solution.py:49
  1025.0 65.7 %all-reduce.37.cloned.1.call-done = (f32[32,1280]{1,0:T(8,128)}, f32[32,1280]{1,0:T(8,128)}, f32[32,1280]{1,0:T(8,128)}, f32[32,1280]{1,0:T(8,128)}) async-done(((f32[32,1280]{1,0:T(8,128)}, f32[32,1280]{1,0:T(8,128)}, f32[32,1280]{1,0:T(8,128)}, f32[32,1280]{1,0:T(8,128)}), (f32[32,1280]{1,0:T(8,128)}, f32[32,1280]{1,0:T(8,128)}, f32[32,1280]{1,0:T(8,128)}, ...) | async-done | bytes 655376 | tf_op jit(solution)/shard_map/psum | solution.py:9
  1125.0 56.5 %all-reduce.29.cloned.1.call-done = f32[32,1280]{1,0:T(8,128)} async-done(((f32[32,1280]{1,0:T(8,128)}), f32[32,1280]{1,0:T(8,128)}) %all-reduce.29.cloned.1.call-update) | async-done | bytes 163856 | tf_op jit(solution)/shard_map/psum | solution.py:48
  1182.9 74.6 %psum.279 = f32[32,32]{0,1:T(8,128)S(1)} all-reduce(f32[32,32]{0,1:T(8,128)S(1)} %convolution_bitcast_fusion.7), channel_id=1, replica_groups=mesh['pr'=16,'pc'=8] {'pr'}, use_global_device_ids=true, to_apply=%region_27.28 | all-reduce | flops 1024 | bytes 8192 | tf_op jit(solution)/shard_map/psum | solution.py:49
  1260.8 79.3 %all-reduce.35.cloned.1.call-done = (f32[32,1280]{1,0:T(8,128)}, f32[32,1280]{1,0:T(8,128)}, f32[32,1280]{1,0:T(8,128)}, f32[32,1280]{1,0:T(8,128)}) async-done(((f32[32,1280]{1,0:T(8,128)}, f32[32,1280]{1,0:T(8,128)}, f32[32,1280]{1,0:T(8,128)}, f32[32,1280]{1,0:T(8,128)}), (f32[32,1280]{1,0:T(8,128)}, f32[32,1280]{1,0:T(8,128)}, f32[32,1280]{1,0:T(8,128)}, ...) | async-done | bytes 655376 | tf_op jit(solution)/shard_map/psum | solution.py:9
  1342.0 14.4 convolution_subtract_fusion.1
  1374.0 57.2 %all-reduce.31.cloned.1.call-done = f32[32,1280]{1,0:T(8,128)} async-done(((f32[32,1280]{1,0:T(8,128)}), f32[32,1280]{1,0:T(8,128)}) %all-reduce.31.cloned.1.call-update) | async-done | bytes 163856 | tf_op jit(solution)/shard_map/psum | solution.py:48
  1432.5 74.9 %psum.285 = f32[32,32]{0,1:T(8,128)S(1)} all-reduce(f32[32,32]{0,1:T(8,128)S(1)} %convolution_bitcast_fusion.6), channel_id=1, replica_groups=mesh['pr'=16,'pc'=8] {'pr'}, use_global_device_ids=true, to_apply=%region_33.34 | all-reduce | flops 1024 | bytes 8192 | tf_op jit(solution)/shard_map/psum | solution.py:49
  1510.9 77.3 %all-reduce.33.cloned.1.call-done = (f32[32,1280]{1,0:T(8,128)}, f32[32,1280]{1,0:T(8,128)}) async-done(((f32[32,1280]{1,0:T(8,128)}, f32[32,1280]{1,0:T(8,128)}), (f32[32,1280]{1,0:T(8,128)}, f32[32,1280]{1,0:T(8,128)})) %all-reduce.33.cloned.1.call-update) | async-done | bytes 327696 | tf_op jit(solution)/shard_map/psum | solution.py:9
  1588.1 15.4 convolution_subtract_fusion
  (120 shorter events, 255.3 us)
Async XLA Ops:
  7.2 252.0 %copy-start.5 = (f32[6,32,32]{2,1,0:T(8,128)S(1)}, f32[6,32,32]{2,1,0:T(8,128)}, u32[]{:S(2)}) copy-start(f32[6,32,32]{2,1,0:T(8,128)} %param.5) | copy-start | bytes 73732
  7.2 101.6 %all-reduce.45.cloned.1.call-start = ((), (), s32[]{:S(2)}) async-start(), calls=%async_computation.12 | async-start | bytes 655360 | tf_op jit(solution)/shard_map/psum | solution.py:9
  23.2 160.1 %all-reduce.21.cloned.1.call-start = ((), (), s32[]{:S(2)}) async-start(), calls=%async_computation | async-start | bytes 327680 | tf_op jit(solution)/shard_map/psum | solution.py:48
  126.0 215.9 %all-reduce.43.cloned.1.call-start = ((), (), s32[]{:S(2)}) async-start(), calls=%async_computation.11 | async-start | bytes 1310720 | tf_op jit(solution)/shard_map/psum | solution.py:9
  262.4 170.6 %all-reduce.23.cloned.1.call-start = ((), (), s32[]{:S(2)}) async-start(), calls=%async_computation.1 | async-start | bytes 327680 | tf_op jit(solution)/shard_map/psum | solution.py:48
  358.3 5.0 copy-start.3
  375.7 216.0 %all-reduce.41.cloned.1.call-start = ((), (), s32[]{:S(2)}) async-start(), calls=%async_computation.10 | async-start | bytes 1310720 | tf_op jit(solution)/shard_map/psum | solution.py:9
  512.1 170.4 %all-reduce.25.cloned.1.call-start = ((), (), s32[]{:S(2)}) async-start(), calls=%async_computation.2 | async-start | bytes 327680 | tf_op jit(solution)/shard_map/psum | solution.py:48
  607.8 5.0 copy-start.2
  625.2 215.9 %all-reduce.39.cloned.1.call-start = ((), (), s32[]{:S(2)}) async-start(), calls=%async_computation.9 | async-start | bytes 1310720 | tf_op jit(solution)/shard_map/psum | solution.py:9
  761.6 170.4 %all-reduce.27.cloned.1.call-start = ((), (), s32[]{:S(2)}) async-start(), calls=%async_computation.3 | async-start | bytes 327680 | tf_op jit(solution)/shard_map/psum | solution.py:48
  857.3 5.0 copy-start.1
  874.7 216.0 %all-reduce.37.cloned.1.call-start = ((), (), s32[]{:S(2)}) async-start(), calls=%async_computation.8 | async-start | bytes 1310720 | tf_op jit(solution)/shard_map/psum | solution.py:9
  1011.1 170.4 %all-reduce.29.cloned.1.call-start = ((), (), s32[]{:S(2)}) async-start(), calls=%async_computation.4 | async-start | bytes 327680 | tf_op jit(solution)/shard_map/psum | solution.py:48
  1106.8 5.0 copy-start
  1124.2 215.9 %all-reduce.35.cloned.1.call-start = ((), (), s32[]{:S(2)}) async-start(), calls=%async_computation.7 | async-start | bytes 1310720 | tf_op jit(solution)/shard_map/psum | solution.py:9
  1260.6 170.6 %all-reduce.31.cloned.1.call-start = ((), (), s32[]{:S(2)}) async-start(), calls=%async_computation.5 | async-start | bytes 327680 | tf_op jit(solution)/shard_map/psum | solution.py:48
  1356.5 5.0 copy-start.4
  1373.9 214.3 %all-reduce.33.cloned.1.call-start = ((), (), s32[]{:S(2)}) async-start(), calls=%async_computation.6 | async-start | bytes 655360 | tf_op jit(solution)/shard_map/psum | solution.py:9
  1510.9 92.7 %copy-start.6 = (f32[6,32,160]{2,1,0:T(8,128)}, f32[6,32,160]{2,1,0:T(8,128)S(1)}, u32[]{:S(2)}) copy-start(f32[6,32,160]{2,1,0:T(8,128)S(1)} %constant_dynamic-update-slice_fusion.12) | copy-start | bytes 368644
Sparse Core Ops, SparseCore 0:
  23.3 85.4 all-reduce.44
  126.1 57.1 all-reduce.20
  262.5 79.3 all-reduce.42
  375.8 57.1 all-reduce.22
  512.2 79.4 all-reduce.40
  625.3 57.1 all-reduce.24
  761.7 79.3 all-reduce.38
  874.8 57.1 all-reduce.26
  1011.2 79.4 all-reduce.36
  1124.3 57.1 all-reduce.28
  1260.7 79.3 all-reduce.34
  1374.0 57.1 all-reduce.30
  1510.7 77.3 all-reduce.32
where the time goes:
time: 1620 us; the launch traced here: 1610 us
  waiting for transfers between devices  819 us (51%)
  blocking collectives  528 us (33%)
  matrix products  192 us (12%)
  local copies, waits for them, and re-layouts  52.1 us (3%)
    psum x7, waiting for transfers between devices, broadcast(): return lax.psum(kept, axis)  479 us
    psum x6, blocking collectives, per_device(): gram_block = lax.psum(contract(v_row, x_row, 1, 1), 'pr')  448 us
    psum x6, waiting for transfers between devices, per_device(): x_row = lax.psum(partial_value, 'pc')  340 us
    dot_general x42, matrix products, contract(): lax.dot_general(left_side, right_side, (((left_dim,), (right_dim,)), ((),...  192 us
    all_gather x6, blocking collectives, per_device(): v_row = lax.all_gather(v_panels[panel], 'pc', axis=1, tiled=True)  80.3 us
  transfers between devices with their start and end apart: 13, of which 13 were waited for; matrix products, arithmetic and copies ran while one was open for 1% of the time, Pallas kernels for 0%

commit v1 on v0

--- a/solution.py
+++ b/solution.py
@@ -45,7 +45,7 @@
         v_col = fetch_v_columns(v_row, col_rank, ratio)
         factor = t_panels[panel]
         partial_value = contract(v_col, matrix, 1, 1)
-        x_row = lax.psum(partial_value, "pc")
+        x_row = lax.all_gather(partial_value, "pc").sum(axis=0)
         gram_block = lax.psum(contract(v_row, x_row, 1, 1), "pr")
         middle = contract(contract(factor, gram_block, 0, 0), factor, 1, 0)
         w_row = contract(factor, x_row, 0, 0) - 0.5 * contract(middle, v_row, 0, 0)

time: 1620 us -> 1430 us (0.88)
  waiting for transfers between devices: 819 us -> 634 us
    psum x6 -> x0, waiting for transfers between devices: 340 us -> none  [per_device(): x_row = lax.psum(partial_value, 'pc')]
    psum x7, waiting for transfers between devices: 479 us -> 567 us  [broadcast(): return lax.psum(kept, axis)]
    all_gather x0 -> x6, waiting for transfers between devices: none -> 65.8 us  [per_device(): x_row = lax.all_gather(partial_value, 'pc').sum(axis=0)]
  transfers between devices with their start and end apart: 13 -> 13, of which waited for: 13 -> 13; matrix products, arithmetic and copies ran while one was open for 1% -> 0% of each run, Pallas kernels for 0% -> 0%
where the time goes in v1:
time: 1430 us
  waiting for transfers between devices  634 us (44%)
  blocking collectives  530 us (37%)
  matrix products  193 us (13%)
  local copies, waits for them, and re-layouts  39.8 us (3%)
  between operations  14.7 us (1%)
    psum x7, waiting for transfers between devices, broadcast(): return lax.psum(kept, axis)  567 us
    psum x6, blocking collectives, per_device(): gram_block = lax.psum(contract(v_row, x_row, 1, 1), 'pr')  448 us
    dot_general x42, matrix products, contract(): lax.dot_general(left_side, right_side, (((left_dim,), (right_dim,)), ((),...  193 us
    all_gather x6, blocking collectives, per_device(): v_row = lax.all_gather(v_panels[panel], 'pc', axis=1, tiled=True)  81.9 us
    all_gather x6, waiting for transfers between devices, per_device(): x_row = lax.all_gather(partial_value, 'pc').sum(axis=0)  65.8 us
    unnamed x31, local copies, waits for them, and re-layouts  31.3 us
  transfers between devices with their start and end apart: 13, of which 13 were waited for; matrix products, arithmetic and copies ran while one was open for 0% of the time, Pallas kernels for 0%

profile of v1, /device:TPU:0, one launch (start us, length us, event | category | flops | bytes accessed | tf_op | source)
XLA Modules:
  0.0 1425.4 jit_solution(1500283033392890727)
XLA Ops:
  8.2 13.8 all-gather
  23.2 85.5 %all-reduce.27.cloned.1.call-done = (f32[32,1280]{1,0:T(8,128)}, f32[32,1280]{1,0:T(8,128)}) async-done(((f32[32,1280]{1,0:T(8,128)}, f32[32,1280]{1,0:T(8,128)}), (f32[32,1280]{1,0:T(8,128)}, f32[32,1280]{1,0:T(8,128)})) %all-reduce.27.cloned.1.call-update) | async-done | bytes 327696 | tf_op jit(solution)/shard_map/psum | solution.py:9
  110.6 15.3 %fusion.109 = f32[32,1280]{1,0:T(8,128)} fusion(f32[32,2560]{1,0:T(8,128)S(1)} %constant_dynamic-update-slice_fusion, f32[1280,2560]{1,0:T(8,128)} %param.3), kind=kOutput, calls=%fused_computation.175 | convolution fusion | flops 1258291200 | bytes 13598720 | tf_op jit(solution)/shard_map/dot_general | solution.py:13
  126.1 13.7 all-gather.2
  151.1 74.7 %psum.212 = f32[32,32]{0,1:T(8,128)S(1)} all-reduce(f32[32,32]{0,1:T(8,128)S(1)} %convolution_bitcast_fusion.11), channel_id=1, replica_groups=mesh['pr'=16,'pc'=8] {'pr'}, use_global_device_ids=true, to_apply=%region_3.4 | all-reduce | flops 1024 | bytes 8192 | tf_op jit(solution)/shard_map/psum | solution.py:49
  228.3 80.5 %all-reduce.25.cloned.1.call-done = (f32[32,1280]{1,0:T(8,128)}, f32[32,1280]{1,0:T(8,128)}, f32[32,1280]{1,0:T(8,128)}, f32[32,1280]{1,0:T(8,128)}) async-done(((f32[32,1280]{1,0:T(8,128)}, f32[32,1280]{1,0:T(8,128)}, f32[32,1280]{1,0:T(8,128)}, f32[32,1280]{1,0:T(8,128)}), (f32[32,1280]{1,0:T(8,128)}, f32[32,1280]{1,0:T(8,128)}, f32[32,1280]{1,0:T(8,128)}, ...) | async-done | bytes 655376 | tf_op jit(solution)/shard_map/psum | solution.py:9
  310.7 14.6 %convolution_subtract_fusion.5 = f32[1280,2560]{1,0:T(8,128)S(1)} fusion(f32[1280,2560]{1,0:T(8,128)} %param.3, f32[32,2560]{1,0:T(8,128)S(1)} %constant_dynamic-update-slice_fusion, f32[32,1280]{1,0:T(8,128)} %get-tuple-element.20, f32[32,1280]{1,0:T(8,128)} %get-tuple-element.21, f32[32,1280]{1,0:T(8,128)S(1)} %get-tuple-element.56, ...), kind=kOutput, calls=%fused_computation.5 | convolution fusion | flops 2520268800 | bytes 27197440 | tf_op jit(solution)/shard_map/dot_general | solution.py:13
  368.3 74.7 %psum.217 = f32[32,32]{0,1:T(8,128)S(1)} all-reduce(f32[32,32]{0,1:T(8,128)S(1)} %convolution_bitcast_fusion.10), channel_id=1, replica_groups=mesh['pr'=16,'pc'=8] {'pr'}, use_global_device_ids=true, to_apply=%region_9.10 | all-reduce | flops 1024 | bytes 8192 | tf_op jit(solution)/shard_map/psum | solution.py:49
  445.0 80.7 %all-reduce.23.cloned.1.call-done = (f32[32,1280]{1,0:T(8,128)}, f32[32,1280]{1,0:T(8,128)}, f32[32,1280]{1,0:T(8,128)}, f32[32,1280]{1,0:T(8,128)}) async-done(((f32[32,1280]{1,0:T(8,128)}, f32[32,1280]{1,0:T(8,128)}, f32[32,1280]{1,0:T(8,128)}, f32[32,1280]{1,0:T(8,128)}), (f32[32,1280]{1,0:T(8,128)}, f32[32,1280]{1,0:T(8,128)}, f32[32,1280]{1,0:T(8,128)}, ...) | async-done | bytes 655376 | tf_op jit(solution)/shard_map/psum | solution.py:9
  527.6 26.4 %convolution_subtract_fusion.4 = f32[1280,2560]{1,0:T(8,128)S(1)} fusion(f32[1280,2560]{1,0:T(8,128)} %copy-done.4, f32[32,2560]{1,0:T(8,128)S(1)} %constant_dynamic-update-slice_fusion.2, f32[32,1280]{1,0:T(8,128)} %get-tuple-element.16, f32[32,1280]{1,0:T(8,128)} %get-tuple-element.17, f32[32,1280]{1,0:T(8,128)S(1)} %get-tuple-element.57, ...), kind=kOutput, calls=%fused_computation.4 | convolution fusion | flops 2520268800 | bytes 27197440 | tf_op jit(solution)/shard_map/dot_general | solution.py:13
  596.9 74.7 %psum.222 = f32[32,32]{0,1:T(8,128)S(1)} all-reduce(f32[32,32]{0,1:T(8,128)S(1)} %convolution_bitcast_fusion.9), channel_id=1, replica_groups=mesh['pr'=16,'pc'=8] {'pr'}, use_global_device_ids=true, to_apply=%region_15.16 | all-reduce | flops 1024 | bytes 8192 | tf_op jit(solution)/shard_map/psum | solution.py:49
  673.6 80.7 %all-reduce.21.cloned.1.call-done = (f32[32,1280]{1,0:T(8,128)}, f32[32,1280]{1,0:T(8,128)}, f32[32,1280]{1,0:T(8,128)}, f32[32,1280]{1,0:T(8,128)}) async-done(((f32[32,1280]{1,0:T(8,128)}, f32[32,1280]{1,0:T(8,128)}, f32[32,1280]{1,0:T(8,128)}, f32[32,1280]{1,0:T(8,128)}), (f32[32,1280]{1,0:T(8,128)}, f32[32,1280]{1,0:T(8,128)}, f32[32,1280]{1,0:T(8,128)}, ...) | async-done | bytes 655376 | tf_op jit(solution)/shard_map/psum | solution.py:9
  756.2 14.7 %convolution_subtract_fusion.3 = f32[1280,2560]{1,0:T(8,128)S(1)} fusion(f32[1280,2560]{1,0:T(8,128)} %copy-done.2, f32[32,2560]{1,0:T(8,128)S(1)} %constant_dynamic-update-slice_fusion.4, f32[32,1280]{1,0:T(8,128)} %get-tuple-element.12, f32[32,1280]{1,0:T(8,128)} %get-tuple-element.13, f32[32,1280]{1,0:T(8,128)S(1)} %get-tuple-element.58, ...), kind=kOutput, calls=%fused_computation.3 | convolution fusion | flops 2520268800 | bytes 27197440 | tf_op jit(solution)/shard_map/dot_general | solution.py:13
  813.9 74.7 %psum.227 = f32[32,32]{0,1:T(8,128)S(1)} all-reduce(f32[32,32]{0,1:T(8,128)S(1)} %convolution_bitcast_fusion.8), channel_id=1, replica_groups=mesh['pr'=16,'pc'=8] {'pr'}, use_global_device_ids=true, to_apply=%region_21.22 | all-reduce | flops 1024 | bytes 8192 | tf_op jit(solution)/shard_map/psum | solution.py:49
  890.6 80.7 %all-reduce.19.cloned.1.call-done = (f32[32,1280]{1,0:T(8,128)}, f32[32,1280]{1,0:T(8,128)}, f32[32,1280]{1,0:T(8,128)}, f32[32,1280]{1,0:T(8,128)}) async-done(((f32[32,1280]{1,0:T(8,128)}, f32[32,1280]{1,0:T(8,128)}, f32[32,1280]{1,0:T(8,128)}, f32[32,1280]{1,0:T(8,128)}), (f32[32,1280]{1,0:T(8,128)}, f32[32,1280]{1,0:T(8,128)}, f32[32,1280]{1,0:T(8,128)}, ...) | async-done | bytes 655376 | tf_op jit(solution)/shard_map/psum | solution.py:9
  973.1 14.4 %convolution_subtract_fusion.2 = f32[1280,2560]{1,0:T(8,128)S(1)} fusion(f32[1280,2560]{1,0:T(8,128)} %copy-done.3, f32[32,2560]{1,0:T(8,128)S(1)} %constant_dynamic-update-slice_fusion.6, f32[32,1280]{1,0:T(8,128)} %get-tuple-element.8, f32[32,1280]{1,0:T(8,128)} %get-tuple-element.9, f32[32,1280]{1,0:T(8,128)S(1)} %get-tuple-element.59, ...), kind=kOutput, calls=%fused_computation.2 | convolution fusion | flops 2520268800 | bytes 27197440 | tf_op jit(solution)/shard_map/dot_general | solution.py:13
  1005.1 13.6 all-gather.10
  1030.5 74.7 %psum.232 = f32[32,32]{0,1:T(8,128)S(1)} all-reduce(f32[32,32]{0,1:T(8,128)S(1)} %convolution_bitcast_fusion.7), channel_id=1, replica_groups=mesh['pr'=16,'pc'=8] {'pr'}, use_global_device_ids=true, to_apply=%region_27.28 | all-reduce | flops 1024 | bytes 8192 | tf_op jit(solution)/shard_map/psum | solution.py:49
  1107.2 80.7 %all-reduce.17.cloned.1.call-done = (f32[32,1280]{1,0:T(8,128)}, f32[32,1280]{1,0:T(8,128)}, f32[32,1280]{1,0:T(8,128)}, f32[32,1280]{1,0:T(8,128)}) async-done(((f32[32,1280]{1,0:T(8,128)}, f32[32,1280]{1,0:T(8,128)}, f32[32,1280]{1,0:T(8,128)}, f32[32,1280]{1,0:T(8,128)}), (f32[32,1280]{1,0:T(8,128)}, f32[32,1280]{1,0:T(8,128)}, f32[32,1280]{1,0:T(8,128)}, ...) | async-done | bytes 655376 | tf_op jit(solution)/shard_map/psum | solution.py:9
  1189.8 14.5 %convolution_subtract_fusion.1 = f32[1280,2560]{1,0:T(8,128)S(1)} fusion(f32[1280,2560]{1,0:T(8,128)} %copy-done.1, f32[32,2560]{1,0:T(8,128)S(1)} %constant_dynamic-update-slice_fusion.8, f32[32,1280]{1,0:T(8,128)} %get-tuple-element.4, f32[32,1280]{1,0:T(8,128)} %get-tuple-element.5, f32[32,1280]{1,0:T(8,128)S(1)} %get-tuple-element.60, ...), kind=kOutput, calls=%fused_computation.1 | convolution fusion | flops 2520268800 | bytes 27197440 | tf_op jit(solution)/shard_map/dot_general | solution.py:13
  1222.0 23.3 %all-gather.29.cloned.1.call-done = f32[256,1280]{1,0:T(8,128)} async-done(((f32[32,1280]{1,0:T(8,128)}), f32[256,1280]{1,0:T(8,128)}) %all-gather.29.cloned.1.call-update) | async-done | bytes 1310736 | tf_op jit(solution)/shard_map/all_gather | solution.py:48
  1247.5 74.8 %psum.237 = f32[32,32]{0,1:T(8,128)S(1)} all-reduce(f32[32,32]{0,1:T(8,128)S(1)} %convolution_bitcast_fusion.6), channel_id=1, replica_groups=mesh['pr'=16,'pc'=8] {'pr'}, use_global_device_ids=true, to_apply=%region_33.34 | all-reduce | flops 1024 | bytes 8192 | tf_op jit(solution)/shard_map/psum | solution.py:49
  1324.5 78.5 %all-reduce.15.cloned.1.call-done = (f32[32,1280]{1,0:T(8,128)}, f32[32,1280]{1,0:T(8,128)}) async-done(((f32[32,1280]{1,0:T(8,128)}, f32[32,1280]{1,0:T(8,128)}), (f32[32,1280]{1,0:T(8,128)}, f32[32,1280]{1,0:T(8,128)})) %all-reduce.15.cloned.1.call-update) | async-done | bytes 327696 | tf_op jit(solution)/shard_map/psum | solution.py:9
  1403.0 15.4 %convolution_subtract_fusion = f32[1280,2560]{1,0:T(8,128)} fusion(f32[1280,2560]{1,0:T(8,128)} %copy-done, f32[32,2560]{1,0:T(8,128)S(1)} %constant_dynamic-update-slice_fusion.10, f32[32,1280]{1,0:T(8,128)} %get-tuple-element.2, f32[32,1280]{1,0:T(8,128)} %get-tuple-element.3, f32[32,1280]{1,0:T(8,128)S(1)} %get-tuple-element.61, f32[32,1280]{1,0:T(8,128)S(1)} %bitcast.180), kind=kOutput, calls=%fused_computation | convolution fusion | flops 2520268800 | bytes 27197440 | tf_op jit(solution)/shard_map/dot_general | solution.py:13
  (126 shorter events, 215.1 us)
Async XLA Ops:
  7.2 218.7 %copy-start.5 = (f32[6,32,32]{2,1,0:T(8,128)S(1)}, f32[6,32,32]{2,1,0:T(8,128)}, u32[]{:S(2)}) copy-start(f32[6,32,32]{2,1,0:T(8,128)} %param.5) | copy-start | bytes 73732
  7.2 101.6 %all-reduce.27.cloned.1.call-start = ((), (), s32[]{:S(2)}) async-start(), calls=%async_computation.12 | async-start | bytes 655360 | tf_op jit(solution)/shard_map/psum | solution.py:9
  23.2 126.1 %all-gather.19.cloned.1.call-start = ((), (), s32[]{:S(2)}) async-start(), calls=%async_computation | async-start | bytes 1474560 | tf_op jit(solution)/shard_map/all_gather | solution.py:48
  126.0 182.9 %all-reduce.25.cloned.1.call-start = ((), (), s32[]{:S(2)}) async-start(), calls=%async_computation.11 | async-start | bytes 1310720 | tf_op jit(solution)/shard_map/psum | solution.py:9
  228.1 138.0 %all-gather.21.cloned.1.call-start = ((), (), s32[]{:S(2)}) async-start(), calls=%async_computation.1 | async-start | bytes 1474560 | tf_op jit(solution)/shard_map/all_gather | solution.py:48
  325.3 5.0 copy-start.4
  342.7 183.0 %all-reduce.23.cloned.1.call-start = ((), (), s32[]{:S(2)}) async-start(), calls=%async_computation.10 | async-start | bytes 1310720 | tf_op jit(solution)/shard_map/psum | solution.py:9
  444.9 149.8 %all-gather.23.cloned.1.call-start = ((), (), s32[]{:S(2)}) async-start(), calls=%async_computation.2 | async-start | bytes 1474560 | tf_op jit(solution)/shard_map/all_gather | solution.py:48
  553.9 5.0 copy-start.2
  571.4 183.0 %all-reduce.21.cloned.1.call-start = ((), (), s32[]{:S(2)}) async-start(), calls=%async_computation.9 | async-start | bytes 1310720 | tf_op jit(solution)/shard_map/psum | solution.py:9
  673.6 138.1 %all-gather.25.cloned.1.call-start = ((), (), s32[]{:S(2)}) async-start(), calls=%async_computation.3 | async-start | bytes 1474560 | tf_op jit(solution)/shard_map/all_gather | solution.py:48
  770.9 5.0 copy-start.3
  788.3 183.0 %all-reduce.19.cloned.1.call-start = ((), (), s32[]{:S(2)}) async-start(), calls=%async_computation.8 | async-start | bytes 1310720 | tf_op jit(solution)/shard_map/psum | solution.py:9
  890.5 137.8 %all-gather.27.cloned.1.call-start = ((), (), s32[]{:S(2)}) async-start(), calls=%async_computation.4 | async-start | bytes 1474560 | tf_op jit(solution)/shard_map/all_gather | solution.py:48
  987.6 5.0 copy-start.1
  1005.0 183.0 %all-reduce.17.cloned.1.call-start = ((), (), s32[]{:S(2)}) async-start(), calls=%async_computation.7 | async-start | bytes 1310720 | tf_op jit(solution)/shard_map/psum | solution.py:9
  1107.2 138.1 %all-gather.29.cloned.1.call-start = ((), (), s32[]{:S(2)}) async-start(), calls=%async_computation.5 | async-start | bytes 1474560 | tf_op jit(solution)/shard_map/all_gather | solution.py:48
  1204.3 5.0 copy-start
  1221.7 181.3 %all-reduce.15.cloned.1.call-start = ((), (), s32[]{:S(2)}) async-start(), calls=%async_computation.6 | async-start | bytes 655360 | tf_op jit(solution)/shard_map/psum | solution.py:9
  1324.5 94.0 %copy-start.6 = (f32[6,32,160]{2,1,0:T(8,128)}, f32[6,32,160]{2,1,0:T(8,128)S(1)}, u32[]{:S(2)}) copy-start(f32[6,32,160]{2,1,0:T(8,128)S(1)} %constant_dynamic-update-slice_fusion.12) | copy-start | bytes 368644
Sparse Core Ops, SparseCore 0:
  23.3 85.4 all-reduce.26
  126.1 23.1 all-gather.18
  228.2 80.6 all-reduce.24
  342.8 23.2 all-gather.20
  445.1 80.5 all-reduce.22
  571.5 23.2 all-gather.22
  673.7 80.5 all-reduce.20
  788.4 23.2 all-gather.24
  890.6 80.5 all-reduce.18
  1005.1 23.1 all-gather.26
  1107.3 80.6 all-reduce.16
  1221.8 23.4 all-gather.28
  1324.4 78.5 all-reduce.14
